TPU v7x, 32 devices: a whole 2x2x4 slice. The times are simulated.
32 devices in a mesh: dp: 2 (over x), expert: 16 (over z, y, core).
Axes of the slice: x: 2, y: 2, z: 4, core: 2. Of those that a mesh axis runs over, the one named last changes fastest.
Arguments:
- tokens: bfloat16 [2048, 2560], P('expert', 'dp'), may hold values from -6 to 6
- cotangent: bfloat16 [2048, 2560], P('expert', 'dp'), may hold values from -6 to 6
- expert_ids: int32 [2048, 6], P('expert'), may hold values from 0 to 15, all different within a row; in each aligned block of 128 rows (0 to 127, 128 to 255, ...) at most 64 rows name the same one
- gate_weights: float32 [2048, 6], P('expert'), may hold values from 0.1 to 0.6
- w_in: bfloat16 [16, 2560, 768], P('expert', 'dp'), may hold values from -0.125 to 0.125
- w_out: bfloat16 [16, 768, 2560], P('expert', None, 'dp'), may hold values from -0.21875 to 0.21875
Outputs:
- mixed_out: bfloat16 [2048, 2560], P('expert', 'dp')
- token_grad: bfloat16 [2048, 2560], P('expert', 'dp')
- w_in_grad: bfloat16 [16, 2560, 768], P('expert', 'dp')
- w_out_grad: bfloat16 [16, 768, 2560], P('expert', None, 'dp')
Inputs may be any that keep to these rules, and one draw needn't show every extreme that they name: `expert_ids`: each row names 6 different experts. Within the rows of one device (aligned blocks of 128 rows) no expert is named more than 64 times, a bound that some block reaches.
All inputs are finite; a program needn't handle non-finite values.
Results may differ from a plain program's by a relative error of at most 0.017.
Values may be sent and summed in bfloat16 or wider, within the bound.
A program may use at most 64 MiB of HBM per device.

v0:
```python
import jax
import jax.numpy as jnp
from jax import lax
from jax.sharding import PartitionSpec as P


def silu_slope(hidden_value):
    logistic = jax.nn.sigmoid(hidden_value)
    return logistic * (1.0 + hidden_value * (1.0 - logistic))


def expert_hidden(rows_x, weight_in):
    partial_sum = jnp.dot(rows_x, weight_in, preferred_element_type=jnp.float32)
    share_sum = lax.psum_scatter(
        partial_sum.astype(jnp.bfloat16), "dp", scatter_dimension=1, tiled=True
    ).astype(jnp.float32)
    share_act = jax.nn.silu(share_sum).astype(jnp.bfloat16)
    return (share_sum, lax.all_gather(share_act, "dp", axis=1, tiled=True))


def expert_slope(rows_dy, weight_out, preact):
    partial_sum = lax.dot_general(
        rows_dy, weight_out, (((1,), (1,)), ((), ())), preferred_element_type=jnp.float32
    )
    share_sum = lax.psum_scatter(
        partial_sum.astype(jnp.bfloat16), "dp", scatter_dimension=1, tiled=True
    ).astype(jnp.float32)
    share_delta = (share_sum * silu_slope(preact)).astype(jnp.bfloat16)
    return lax.all_gather(share_delta, "dp", axis=1, tiled=True)


def local(tokens, cotangent, expert_ids, gate_weights, w_in, w_out):
    experts = lax.axis_size("expert")
    tok_rows, quarter = tokens.shape
    choose_count = expert_ids.shape[1]
    capacity = max(2, 4 * tok_rows * choose_count // (3 * experts))
    assign = tok_rows * choose_count
    flat_ids = expert_ids.reshape(-1)
    onehot = (flat_ids[:, None] == jnp.arange(experts, dtype=jnp.int32)[None, :]).astype(jnp.int32)
    earlier = jnp.sum((jnp.cumsum(onehot, axis=0) - onehot) * onehot, axis=1)
    slot_index = flat_ids * capacity + earlier
    source = (
        jnp.full((experts * capacity,), assign, jnp.int32)
        .at[slot_index]
        .set(jnp.arange(assign, dtype=jnp.int32))
    )
    token_of = source // choose_count
    zero_row = jnp.zeros((1, quarter), jnp.bfloat16)
    send_x = jnp.concatenate([tokens, zero_row], 0)[token_of].reshape(experts, capacity, quarter)
    slot_gate = jnp.concatenate([gate_weights.reshape(-1), jnp.zeros((1,), jnp.float32)], 0)[source]
    picked_dy = jnp.concatenate([cotangent, zero_row], 0)[token_of]
    send_dy = (
        (slot_gate[:, None] * picked_dy.astype(jnp.float32))
        .astype(jnp.bfloat16)
        .reshape(experts, capacity, quarter)
    )
    weight_in = w_in[0]
    weight_out = w_out[0]
    arrived_x = lax.all_to_all(send_x, "expert", split_axis=0, concat_axis=0, tiled=True)
    rows_x = arrived_x.reshape(-1, quarter)
    preact, activation = expert_hidden(rows_x, weight_in)
    out_rows = jnp.dot(activation, weight_out, preferred_element_type=jnp.float32).astype(
        jnp.bfloat16
    )
    rows_x, preact, activation, out_rows = (
        rows_x,
        preact,
        activation,
        out_rows.reshape(experts, capacity, quarter),
    )
    returned_out = lax.all_to_all(out_rows, "expert", split_axis=0, concat_axis=0, tiled=True)
    arrived_dy = lax.all_to_all(send_dy, "expert", split_axis=0, concat_axis=0, tiled=True)
    rows_dy = arrived_dy.reshape(-1, quarter)
    delta_hidden = expert_slope(rows_dy, weight_out, preact)
    out_grad = lax.dot_general(
        activation, rows_dy, (((0,), (0,)), ((), ())), preferred_element_type=jnp.float32
    ).astype(jnp.bfloat16)
    in_grad = lax.dot_general(
        rows_x, delta_hidden, (((0,), (0,)), ((), ())), preferred_element_type=jnp.float32
    ).astype(jnp.bfloat16)
    back_rows = lax.dot_general(
        delta_hidden, weight_in, (((1,), (1,)), ((), ())), preferred_element_type=jnp.float32
    ).astype(jnp.bfloat16)
    in_grad, out_grad, back_rows = (
        in_grad[None],
        out_grad[None],
        back_rows.reshape(experts, capacity, quarter),
    )
    returned_back = lax.all_to_all(back_rows, "expert", split_axis=0, concat_axis=0, tiled=True)

    def gather_rows(returned):
        flat_rows = returned.reshape(experts * capacity, quarter)
        return flat_rows[slot_index].astype(jnp.float32).reshape(tok_rows, choose_count, quarter)

    mixed_out = jnp.sum(gather_rows(returned_out) * gate_weights[:, :, None], axis=1).astype(
        jnp.bfloat16
    )
    token_grad = jnp.sum(gather_rows(returned_back), axis=1).astype(jnp.bfloat16)
    return (mixed_out, token_grad, in_grad, out_grad)


def solution(mesh):
    in_specs = (
        P("expert", "dp"),
        P("expert", "dp"),
        P("expert", None),
        P("expert", None),
        P("expert", "dp", None),
        P("expert", None, "dp"),
    )
    out_specs = (
        P("expert", "dp"),
        P("expert", "dp"),
        P("expert", "dp", None),
        P("expert", None, "dp"),
    )
    return jax.shard_map(local, mesh=mesh, in_specs=in_specs, out_specs=out_specs, check_vma=False)
```

profile of v0, /device:TPU:13, one launch (start us, length us, event | category | flops | bytes accessed | tf_op | source)
XLA Modules:
  0.0 386.5 jit_solution(10710059806611601516)
XLA Ops:
  10.3 1.7 reduce-window.6
  12.4 3.4 scatter_custom_fusion
  15.9 4.5 %gather_fusion.2 = f32[1024]{0:T(1024)S(1)} fusion(f32[769]{0:T(1024)S(1)} %pad_maximum_fusion, s32[1024]{0:T(1024)S(1)} %get-tuple-element.6), kind=kCustom, calls=%fused_computation.2 | custom fusion | bytes 12288 | tf_op jit(solution)/shard_map/gather | solution.py:50
  20.5 5.5 %gather_fusion.3 = bf16[1024,1280]{1,0:T(8,128)(2,1)} fusion(bf16[129,1280]{1,0:T(8,128)(2,1)S(1)} %concatenate.11, s32[1024]{0:T(1024)S(1)} %get-tuple-element.7), kind=kCustom, calls=%fused_computation.3 | custom fusion | bytes 5246976 | tf_op jit(solution)/shard_map/gather | solution.py:51
  26.0 3.8 fusion
  29.8 6.7 %all-to-all-start.2 = ((bf16[16,64,1280]{2,1,0:T(8,128)(2,1)}), bf16[16,64,1280]{2,1,0:T(8,128)(2,1)}, u32[]{:S(2)}, u32[]{:S(2)}) async-start(bf16[16,64,1280]{2,1,0:T(8,128)(2,1)} %fusion), calls=%async_computation.2 | async-start | bytes 5242880 | tf_op jit(solution)/shard_map/all_to_all | solution.py:72
  36.4 5.5 %gather_fusion = bf16[1024,1280]{1,0:T(8,128)(2,1)} fusion(bf16[129,1280]{1,0:T(8,128)(2,1)S(1)} %concatenate.9, s32[1024]{0:T(1024)S(1)} %get-tuple-element.7), kind=kCustom, calls=%fused_computation | custom fusion | bytes 5246976 | tf_op jit(solution)/shard_map/gather | solution.py:49
  41.9 53.3 %all-to-all-done.2 = bf16[16,64,1280]{2,1,0:T(8,128)(2,1)} async-done(((bf16[16,64,1280]{2,1,0:T(8,128)(2,1)}), bf16[16,64,1280]{2,1,0:T(8,128)(2,1)}, u32[]{:S(2)}, u32[]{:S(2)}) %all-to-all-start.2) | async-done | bytes 2621472 | tf_op jit(solution)/shard_map/all_to_all | solution.py:72
  95.2 4.8 %all-to-all-start = ((bf16[16,64,1280]{2,1,0:T(8,128)(2,1)}), bf16[16,64,1280]{2,1,0:T(8,128)(2,1)}, u32[]{:S(2)}, u32[]{:S(2)}) async-start(bf16[16,64,1280]{2,1,0:T(8,128)(2,1)} %bitcast.60), calls=%async_computation | async-start | bytes 5242880 | tf_op jit(solution)/shard_map/all_to_all | solution.py:59
  100.0 4.0 %fusion.12 = bf16[1024,768]{1,0:T(8,128)(2,1)S(1)} fusion(bf16[1024,1280]{1,0:T(8,128)(2,1)} %bitcast.8, bf16[1,768,1280]{2,1,0:T(8,128)(2,1)S(1)} %copy-done), kind=kOutput, calls=%fused_computation.25 | convolution fusion | flops 2014052352 | bytes 6160384 | tf_op jit(solution)/shard_map/dot_general | solution.py:22
  104.0 1.6 copy.25
  105.7 53.0 %all-to-all-done = bf16[16,64,1280]{2,1,0:T(8,128)(2,1)} async-done(((bf16[16,64,1280]{2,1,0:T(8,128)(2,1)}), bf16[16,64,1280]{2,1,0:T(8,128)(2,1)}, u32[]{:S(2)}, u32[]{:S(2)}) %all-to-all-start) | async-done | bytes 2621472 | tf_op jit(solution)/shard_map/all_to_all | solution.py:59
  158.7 4.5 %fusion.9 = bf16[1024,768]{1,0:T(8,128)(2,1)S(1)} fusion(bf16[1024,1280]{1,0:T(8,128)(2,1)} %bitcast.2, bf16[1,1280,768]{2,1,0:T(8,128)(2,1)} %param.10), kind=kOutput, calls=%fused_computation.24 | convolution fusion | flops 2014052352 | bytes 6160384 | tf_op jit(solution)/shard_map/dot_general | solution.py:13
  163.2 1.6 copy.23
  166.5 24.0 %reduce-scatter.7.cloned.1.call-done = bf16[384,1024]{1,0:T(8,128)(2,1)} async-done(((bf16[768,1024]{1,0:T(8,128)(2,1)}), bf16[384,1024]{1,0:T(8,128)(2,1)}) %reduce-scatter.7.cloned.1.call-update) | async-done | bytes 786448
  191.9 1.9 fusion.22
  193.8 27.4 %all-gather.3.cloned.1.call-done = bf16[1024,768]{1,0:T(8,128)(2,1)} async-done(((bf16[1024,384]{1,0:T(8,128)(2,1)}), bf16[1024,768]{1,0:T(8,128)(2,1)}) %all-gather.3.cloned.1.call-update) | async-done | bytes 1572880 | tf_op jit(solution)/shard_map/all_gather | solution.py:18
  221.2 5.2 %convolution_convert_fusion.1 = bf16[1024,1280]{1,0:T(8,128)(2,1)} fusion(bf16[1024,768]{1,0:T(8,128)(2,1)} %all-gather.3.cloned.1.call-done, bf16[1,768,1280]{2,1,0:T(8,128)(2,1)S(1)} %copy-done), kind=kOutput, calls=%fused_computation.10 | convolution fusion | flops 2014576640 | bytes 6160384 | tf_op jit(solution)/shard_map/dot_general | solution.py:62
  226.4 6.5 %all-to-all-start.1 = ((bf16[16,64,1280]{2,1,0:T(8,128)(2,1)}), bf16[16,64,1280]{2,1,0:T(8,128)(2,1)}, u32[]{:S(2)}, u32[]{:S(2)}) async-start(bf16[16,64,1280]{2,1,0:T(8,128)(2,1)} %bitcast.64), calls=%async_computation.1 | async-start | bytes 5242880 | tf_op jit(solution)/shard_map/all_to_all | solution.py:71
  233.4 28.8 %all-gather.5.cloned.1.call-done = bf16[1024,768]{1,0:T(8,128)(2,1)} async-done(((bf16[1024,384]{1,0:T(8,128)(2,1)}), bf16[1024,768]{1,0:T(8,128)(2,1)}) %all-gather.5.cloned.1.call-update) | async-done | bytes 1572880 | tf_op jit(solution)/shard_map/all_gather | solution.py:29
  262.2 5.8 %convolution_convert_fusion = bf16[1024,1280]{1,0:T(8,128)(2,1)} fusion(bf16[1024,768]{1,0:T(8,128)(2,1)} %all-gather.5.cloned.1.call-done, bf16[1,1280,768]{2,1,0:T(8,128)(2,1)} %param.10), kind=kOutput, calls=%fused_computation.9 | convolution fusion | flops 2014576640 | bytes 6160384 | tf_op jit(solution)/shard_map/dot_general | solution.py:81
  268.0 23.6 %all-to-all-done.1 = bf16[16,64,1280]{2,1,0:T(8,128)(2,1)} async-done(((bf16[16,64,1280]{2,1,0:T(8,128)(2,1)}), bf16[16,64,1280]{2,1,0:T(8,128)(2,1)}, u32[]{:S(2)}, u32[]{:S(2)}) %all-to-all-start.1) | async-done | bytes 2621472 | tf_op jit(solution)/shard_map/all_to_all | solution.py:71
  291.6 4.8 %all-to-all-start.3 = ((bf16[16,64,1280]{2,1,0:T(8,128)(2,1)}), bf16[16,64,1280]{2,1,0:T(8,128)(2,1)}, u32[]{:S(2)}, u32[]{:S(2)}) async-start(bf16[16,64,1280]{2,1,0:T(8,128)(2,1)} %bitcast.65), calls=%async_computation.3 | async-start | bytes 5242880 | tf_op jit(solution)/shard_map/all_to_all | solution.py:89
  296.4 5.9 %fusion.1 = bf16[1,1280,768]{2,1,0:T(8,128)(2,1)} fusion(bf16[1024,1280]{1,0:T(8,128)(2,1)} %bitcast.2, bf16[1024,768]{1,0:T(8,128)(2,1)} %all-gather.5.cloned.1.call-done), kind=kOutput, calls=%fused_computation.13 | convolution fusion | flops 2014248960 | bytes 6160384 | tf_op jit(solution)/shard_map/dot_general | solution.py:78
  302.3 5.3 %fusion.2 = bf16[1,768,1280]{2,1,0:T(8,128)(2,1)} fusion(bf16[1024,768]{1,0:T(8,128)(2,1)S(1)} %copy-done.5, bf16[1024,1280]{1,0:T(8,128)(2,1)} %bitcast.8), kind=kOutput, calls=%fused_computation.14 | convolution fusion | flops 2014248960 | bytes 6160384 | tf_op jit(solution)/shard_map/dot_general | solution.py:75
  307.5 7.3 %gather_fusion.1 = bf16[768,1280]{1,0:T(8,128)(2,1)} fusion(bf16[1024,1280]{1,0:T(8,128)(2,1)} %bitcast.6, s32[1024]{0:T(1024)S(1)} %pad_clamp_fusion), kind=kCustom, calls=%fused_computation.1 | custom fusion | bytes 3935232 | tf_op jit(solution)/shard_map/gather | solution.py:93
  314.8 40.3 %all-to-all-done.3 = bf16[16,64,1280]{2,1,0:T(8,128)(2,1)} async-done(((bf16[16,64,1280]{2,1,0:T(8,128)(2,1)}), bf16[16,64,1280]{2,1,0:T(8,128)(2,1)}, u32[]{:S(2)}, u32[]{:S(2)}) %all-to-all-start.3) | async-done | bytes 2621472 | tf_op jit(solution)/shard_map/all_to_all | solution.py:89
  355.2 7.3 %gather_fusion.4 = bf16[768,1280]{1,0:T(8,128)(2,1)} fusion(bf16[1024,1280]{1,0:T(8,128)(2,1)} %bitcast.10, s32[1024]{0:T(1024)S(1)} %pad_clamp_fusion), kind=kCustom, calls=%fused_computation.4 | custom fusion | bytes 3935232 | tf_op jit(solution)/shard_map/gather | solution.py:93
  362.4 4.1 %gather.22 = bf16[128,6,1280]{2,1,0:T(8,128)(2,1)} reshape(bf16[768,1280]{1,0:T(8,128)(2,1)} %gather_fusion.4) | data formatting | bytes 3932160 | tf_op jit(solution)/shard_map/gather | solution.py:93
  366.5 4.1 %reduce_sum.35 = bf16[128,1280]{1,0:T(8,128)(2,1)} reduce(bf16[128,6,1280]{2,1,0:T(8,128)(2,1)} %gather.22, bf16[]{:T(256)} %constant.13.clone.1), dimensions={1}, to_apply=%region_7.8 | reduce | flops 819200 | bytes 2293762 | tf_op jit(solution)/shard_map/reduce_sum | solution.py:98
  370.6 4.5 %reshape.104 = f32[128,6,1280]{2,1,0:T(8,128)} reshape(bf16[768,1280]{1,0:T(8,128)(2,1)} %gather_fusion.1) | data formatting | bytes 5898240 | tf_op jit(solution)/shard_map/convert_element_type | solution.py:93
  375.1 4.9 %multiply_reduce_fusion = bf16[128,1280]{1,0:T(8,128)(2,1)} fusion(f32[128,6,1280]{2,1,0:T(8,128)} %reshape.104, f32[128,6]{1,0:T(8,128)S(1)} %copy-done.2), kind=kLoop, calls=%fused_computation.8 | loop fusion | flops 1802240 | bytes 4262912 | tf_op jit(solution)/shard_map/reduce_sum | solution.py:95
  (43 shorter events, 7.4 us)
Async XLA Ops:
  7.2 92.8 %copy-start = (bf16[1,768,1280]{2,1,0:T(8,128)(2,1)S(1)}, bf16[1,768,1280]{2,1,0:T(8,128)(2,1)}, u32[]{:S(2)}) copy-start(bf16[1,768,1280]{2,1,0:T(8,128)(2,1)} %param.11) | copy-start | bytes 5898244
  10.1 5.7 %copy-start.1 = (f32[128,6]{1,0:T(8,128)}, f32[128,6]{1,0:T(8,128)S(1)}, u32[]{:S(2)}) copy-start(f32[128,6]{1,0:T(8,128)S(1)} %copy.21) | copy-start | bytes 9220
  15.9 4.6 %copy-start.3 = (bf16[128,1280]{1,0:T(8,128)(2,1)S(1)}, bf16[128,1280]{1,0:T(8,128)(2,1)}, u32[]{:S(2)}) copy-start(bf16[128,1280]{1,0:T(8,128)(2,1)} %param.7) | copy-start | bytes 983044
  29.7 6.7 %copy-start.4 = (bf16[128,1280]{1,0:T(8,128)(2,1)S(1)}, bf16[128,1280]{1,0:T(8,128)(2,1)}, u32[]{:S(2)}) copy-start(bf16[128,1280]{1,0:T(8,128)(2,1)} %param.6) | copy-start | bytes 983044
  29.8 65.4 %all-to-all-start.2 = ((bf16[16,64,1280]{2,1,0:T(8,128)(2,1)}), bf16[16,64,1280]{2,1,0:T(8,128)(2,1)}, u32[]{:S(2)}, u32[]{:S(2)}) async-start(bf16[16,64,1280]{2,1,0:T(8,128)(2,1)} %fusion), calls=%async_computation.2 | async-start | bytes 5242880 | tf_op jit(solution)/shard_map/all_to_all | solution.py:72
  95.2 63.5 %all-to-all-start = ((bf16[16,64,1280]{2,1,0:T(8,128)(2,1)}), bf16[16,64,1280]{2,1,0:T(8,128)(2,1)}, u32[]{:S(2)}, u32[]{:S(2)}) async-start(bf16[16,64,1280]{2,1,0:T(8,128)(2,1)} %bitcast.60), calls=%async_computation | async-start | bytes 5242880 | tf_op jit(solution)/shard_map/all_to_all | solution.py:59
  99.9 65.0 %reduce-scatter.9.cloned.1.call-start = ((), (), s32[]{:S(2)}) async-start(), calls=%async_computation.9 | async-start | bytes 2359296
  105.6 84.8 %reduce-scatter.7.cloned.1.call-start = ((), (), s32[]{:S(2)}) async-start(), calls=%async_computation.8 | async-start | bytes 2359296
  164.9 56.3 %all-gather.3.cloned.1.call-start = ((), (), s32[]{:S(2)}) async-start(), calls=%async_computation.6 | async-start | bytes 2359296 | tf_op jit(solution)/shard_map/all_gather | solution.py:18
  226.4 65.3 %all-to-all-start.1 = ((bf16[16,64,1280]{2,1,0:T(8,128)(2,1)}), bf16[16,64,1280]{2,1,0:T(8,128)(2,1)}, u32[]{:S(2)}, u32[]{:S(2)}) async-start(bf16[16,64,1280]{2,1,0:T(8,128)(2,1)} %bitcast.64), calls=%async_computation.1 | async-start | bytes 5242880 | tf_op jit(solution)/shard_map/all_to_all | solution.py:71
  232.9 29.3 %all-gather.5.cloned.1.call-start = ((), (), s32[]{:S(2)}) async-start(), calls=%async_computation.7 | async-start | bytes 2359296 | tf_op jit(solution)/shard_map/all_gather | solution.py:29
  291.6 63.5 %all-to-all-start.3 = ((bf16[16,64,1280]{2,1,0:T(8,128)(2,1)}), bf16[16,64,1280]{2,1,0:T(8,128)(2,1)}, u32[]{:S(2)}, u32[]{:S(2)}) async-start(bf16[16,64,1280]{2,1,0:T(8,128)(2,1)} %bitcast.65), calls=%async_computation.3 | async-start | bytes 5242880 | tf_op jit(solution)/shard_map/all_to_all | solution.py:89
  296.4 5.9 %copy-start.5 = (bf16[1024,768]{1,0:T(8,128)(2,1)S(1)}, bf16[1024,768]{1,0:T(8,128)(2,1)}, u32[]{:S(2)}) copy-start(bf16[1024,768]{1,0:T(8,128)(2,1)} %all-gather.3.cloned.1.call-done) | copy-start | bytes 4718596
  370.6 4.5 %copy-start.2 = (f32[128,6]{1,0:T(8,128)S(1)}, f32[128,6]{1,0:T(8,128)}, u32[]{:S(2)}) copy-start(f32[128,6]{1,0:T(8,128)} %copy-done.1) | copy-start | bytes 9220
Sparse Core Ops, SparseCore 0:
  105.7 26.5 reduce-scatter.8
  165.0 25.3 reduce-scatter.6
  194.0 27.1 all-gather.2
  235.5 26.6 all-gather.4
where the time goes:
time: 387 us
  waiting for transfers between devices  251 us (65%)
  local copies, waits for them, and re-layouts  50.9 us (13%)
  matrix products  30.5 us (8%)
  starting transfers between devices  22.9 us (6%)
  other arithmetic  17.3 us (4%)
  between operations  14 us (4%)
    all_to_all x1, waiting for transfers between devices, local(): lax.all_to_all(send_dy, 'expert', split_axis=0, concat_axis=0, tiled=True)  53.3 us
    all_to_all x1, waiting for transfers between devices, local(): lax.all_to_all(send_x, 'expert', split_axis=0, concat_axis=0, tiled=True)  53 us
    all_to_all x1, waiting for transfers between devices, local(): lax.all_to_all(back_rows, 'expert', split_axis=0, concat_axis=0, tiled=True)  40.3 us
    all_gather x1, waiting for transfers between devices, expert_slope(): return lax.all_gather(share_delta, 'dp', axis=1, tiled=True)  28.8 us
    all_gather x1, waiting for transfers between devices, expert_hidden(): return (share_sum, lax.all_gather(share_act, 'dp', axis=1, tiled=True))  27.4 us
    unnamed x6, waiting for transfers between devices  24.6 us
    all_to_all x1, waiting for transfers between devices, local(): lax.all_to_all(out_rows, 'expert', split_axis=0, concat_axis=0, tiled=True)  23.6 us
    gather x3, local copies, waits for them, and re-layouts, gather_rows(): flat_rows[slot_index].astype(jnp.float32)  18.6 us
  transfers between devices with their start and end apart: 8, of which 7 were waited for; matrix products, arithmetic and copies ran while one was open for 11% of the time, Pallas kernels for 0%

commit v1 on v0

--- a/solution.py
+++ b/solution.py
@@ -1,7 +1,30 @@
+import functools
 import jax
 import jax.numpy as jnp
 from jax import lax
 from jax.sharding import PartitionSpec as P
+
+
+def space_lift(chunk, on_dim, dim_i):
+    z2 = lax.axis_size("expert")
+    latest = lax.axis_index("expert")
+    placed, x_new = (z2, latest)
+    block_last = chunk.shape[on_dim] // placed
+    local_next = jnp.roll(chunk, -x_new * block_last, on_dim)
+    field_out = lax.slice_in_dim(local_next, 0, block_last, axis=on_dim)
+    by_rank = [field_out]
+    for j0 in tuple(range(1, placed)):
+        tmp = lax.slice_in_dim(local_next, j0 * block_last, (j0 + 1) * block_last, axis=on_dim)
+        by_rank.append(
+            lax.ppermute(
+                tmp, axis_name="expert", perm=[(b, (b + j0) % placed) for b in range(placed)]
+            )
+        )
+    known = jnp.concatenate(by_rank[::-1], axis=dim_i)
+    return jnp.roll(known, (x_new + 1) * by_rank[0].shape[dim_i], axis=dim_i)
+
+
+use_the_groups = functools.partial(space_lift, on_dim=0, dim_i=0)
 
 
 def silu_slope(hidden_value):
@@ -56,7 +79,7 @@
     )
     weight_in = w_in[0]
     weight_out = w_out[0]
-    arrived_x = lax.all_to_all(send_x, "expert", split_axis=0, concat_axis=0, tiled=True)
+    arrived_x = use_the_groups(send_x)
     rows_x = arrived_x.reshape(-1, quarter)
     preact, activation = expert_hidden(rows_x, weight_in)
     out_rows = jnp.dot(activation, weight_out, preferred_element_type=jnp.float32).astype(

time: 387 us -> 450 us (1.16)
  waiting for transfers between devices: 251 us -> 286 us
  starting transfers between devices: 22.9 us -> 44.6 us
  local copies, waits for them, and re-layouts: 50.9 us -> 56.8 us
    ppermute x0 -> x15, waiting for transfers between devices: none -> 112 us  [space_lift(): lax.ppermute(tmp, axis_name='expert', perm=[(b, (b + j0) % placed) for b...]
    all_to_all x1, waiting for transfers between devices: 53.3 us -> 0.01 us  [local(): lax.all_to_all(send_dy, 'expert', split_axis=0, concat_axis=0, tiled=True)]
    all_to_all x1 -> x0, waiting for transfers between devices: 53 us -> none  [local(): lax.all_to_all(send_x, 'expert', split_axis=0, concat_axis=0, tiled=True)]
    unnamed x6, waiting for transfers between devices: 24.6 us -> 50.8 us
    ppermute x0 -> x15, starting transfers between devices: none -> 24.5 us  [space_lift(): lax.ppermute(tmp, axis_name='expert', perm=[(b, (b + j0) % placed) for b...]
    unnamed x18 -> x49, local copies, waits for them, and re-layouts: 7.84 us -> 15.6 us
    gather x3, local copies, waits for them, and re-layouts: 18.6 us -> 13.6 us  [gather_rows(): flat_rows[slot_index].astype(jnp.float32)]
    all_to_all x1 -> x0, starting transfers between devices: 4.78 us -> none  [local(): lax.all_to_all(send_x, 'expert', split_axis=0, concat_axis=0, tiled=True)]
  transfers between devices with their start and end apart: 8 -> 22, of which waited for: 7 -> 16; matrix products, arithmetic and copies ran while one was open for 11% -> 12% of each run, Pallas kernels for 0% -> 0%
where the time goes in v1:
time: 450 us; the launch traced here: 449 us
  waiting for transfers between devices  286 us (64%)
  local copies, waits for them, and re-layouts  56.8 us (13%)
  starting transfers between devices  44.6 us (10%)
  matrix products  28.2 us (6%)
  other arithmetic  19.2 us (4%)
  between operations  14.1 us (3%)
    ppermute x15, waiting for transfers between devices, space_lift(): lax.ppermute(tmp, axis_name='expert', perm=[(b, (b + j0) % placed) for b...  112 us
    unnamed x6, waiting for transfers between devices  50.8 us
    all_to_all x1, waiting for transfers between devices, local(): lax.all_to_all(back_rows, 'expert', split_axis=0, concat_axis=0, tiled=True)  43.9 us
    all_gather x1, waiting for transfers between devices, expert_slope(): return lax.all_gather(share_delta, 'dp', axis=1, tiled=True)  28.8 us
    all_gather x1, waiting for transfers between devices, expert_hidden(): return (share_sum, lax.all_gather(share_act, 'dp', axis=1, tiled=True))  27.3 us
    ppermute x15, starting transfers between devices, space_lift(): lax.ppermute(tmp, axis_name='expert', perm=[(b, (b + j0) % placed) for b...  24.5 us
    all_to_all x1, waiting for transfers between devices, local(): lax.all_to_all(out_rows, 'expert', split_axis=0, concat_axis=0, tiled=True)  23.5 us
    unnamed x49, local copies, waits for them, and re-layouts  15.6 us
  transfers between devices with their start and end apart: 22, of which 16 were waited for; matrix products, arithmetic and copies ran while one was open for 12% of the time, Pallas kernels for 0%

profile of v1, /device:TPU:13, one launch (start us, length us, event | category | flops | bytes accessed | tf_op | source)
XLA Modules:
  0.0 449.4 jit_solution(4815344646418998919)
XLA Ops:
  15.9 5.5 %gather_fusion = bf16[1024,1280]{1,0:T(8,128)(2,1)} fusion(bf16[129,1280]{1,0:T(8,128)(2,1)S(1)} %concatenate.15, s32[1024]{0:T(1024)S(1)} %get-tuple-element.23), kind=kCustom, calls=%fused_computation | custom fusion | bytes 5246976 | tf_op jit(solution)/shard_map/gather | solution.py:72
  28.4 4.5 %gather_fusion.2 = f32[1024]{0:T(1024)S(1)} fusion(f32[769]{0:T(1024)S(1)} %pad_maximum_fusion, s32[1024]{0:T(1024)S(1)} %get-tuple-element.22), kind=kCustom, calls=%fused_computation.2 | custom fusion | bytes 12288 | tf_op jit(solution)/shard_map/gather | solution.py:73
  33.0 5.5 %gather_fusion.3 = bf16[1024,1280]{1,0:T(8,128)(2,1)} fusion(bf16[129,1280]{1,0:T(8,128)(2,1)S(1)} %concatenate.18, s32[1024]{0:T(1024)S(1)} %get-tuple-element.23), kind=kCustom, calls=%fused_computation.3 | custom fusion | bytes 5246976 | tf_op jit(solution)/shard_map/gather | solution.py:74
  42.2 8.5 %all-to-all-start.1 = ((bf16[16,64,1280]{2,1,0:T(8,128)(2,1)}), bf16[16,64,1280]{2,1,0:T(8,128)(2,1)}, u32[]{:S(2)}, u32[]{:S(2)}) async-start(bf16[16,64,1280]{2,1,0:T(8,128)(2,1)} %fusion), calls=%async_computation.1 | async-start | bytes 5242880 | tf_op jit(solution)/shard_map/all_to_all | solution.py:95
  56.3 61.6 %collective-permute-done.1 = bf16[1,64,1280]{2,1,0:T(8,128)(2,1)S(1)} collective-permute-done((bf16[1,64,1280]{2,1,0:T(8,128)(2,1)}, bf16[1,64,1280]{2,1,0:T(8,128)(2,1)S(1)}, u32[]{:S(2)}, u32[]{:S(2)}) %collective-permute-start.1) | collective-permute-done | bytes 163872 | tf_op jit(solution)/shard_map/ppermute | solution.py:19
  117.9 5.8 %collective-permute-done.2 = bf16[1,64,1280]{2,1,0:T(8,128)(2,1)S(1)} collective-permute-done((bf16[1,64,1280]{2,1,0:T(8,128)(2,1)}, bf16[1,64,1280]{2,1,0:T(8,128)(2,1)S(1)}, u32[]{:S(2)}, u32[]{:S(2)}) %collective-permute-start.2) | collective-permute-done | bytes 163872 | tf_op jit(solution)/shard_map/ppermute | solution.py:19
  123.7 4.9 %collective-permute-done.3 = bf16[1,64,1280]{2,1,0:T(8,128)(2,1)S(1)} collective-permute-done((bf16[1,64,1280]{2,1,0:T(8,128)(2,1)}, bf16[1,64,1280]{2,1,0:T(8,128)(2,1)S(1)}, u32[]{:S(2)}, u32[]{:S(2)}) %collective-permute-start.3) | collective-permute-done | bytes 163872 | tf_op jit(solution)/shard_map/ppermute | solution.py:19
  130.4 5.9 %collective-permute-done.4 = bf16[1,64,1280]{2,1,0:T(8,128)(2,1)S(1)} collective-permute-done((bf16[1,64,1280]{2,1,0:T(8,128)(2,1)}, bf16[1,64,1280]{2,1,0:T(8,128)(2,1)S(1)}, u32[]{:S(2)}, u32[]{:S(2)}) %collective-permute-start.4) | collective-permute-done | bytes 163872 | tf_op jit(solution)/shard_map/ppermute | solution.py:19
  137.5 6.5 %collective-permute-done.5 = bf16[1,64,1280]{2,1,0:T(8,128)(2,1)S(1)} collective-permute-done((bf16[1,64,1280]{2,1,0:T(8,128)(2,1)}, bf16[1,64,1280]{2,1,0:T(8,128)(2,1)S(1)}, u32[]{:S(2)}, u32[]{:S(2)}) %collective-permute-start.5) | collective-permute-done | bytes 163872 | tf_op jit(solution)/shard_map/ppermute | solution.py:19
  144.0 6.5 %collective-permute-done.6 = bf16[1,64,1280]{2,1,0:T(8,128)(2,1)S(1)} collective-permute-done((bf16[1,64,1280]{2,1,0:T(8,128)(2,1)S(1)}, bf16[1,64,1280]{2,1,0:T(8,128)(2,1)S(1)}, u32[]{:S(2)}, u32[]{:S(2)}) %collective-permute-start.6) | collective-permute-done | bytes 163872 | tf_op jit(solution)/shard_map/ppermute | solution.py:19
  150.5 6.2 %collective-permute-start.7 = (bf16[1,64,1280]{2,1,0:T(8,128)(2,1)S(1)}, bf16[1,64,1280]{2,1,0:T(8,128)(2,1)S(1)}, u32[]{:S(2)}, u32[]{:S(2)}) collective-permute-start(bf16[1,64,1280]{2,1,0:T(8,128)(2,1)S(1)} %copy-done.9), channel_id=1, source_target_pairs={{0,8},{1,9},{2,10},{3,11},{4,12},{5,13},{6,14},{7,15},{8,0},{9,1},... | collective-permute-start | bytes 491528 | tf_op jit(solution)/shard_map/ppermute | solution.py:19
  156.8 6.2 %collective-permute-done.7 = bf16[1,64,1280]{2,1,0:T(8,128)(2,1)S(1)} collective-permute-done((bf16[1,64,1280]{2,1,0:T(8,128)(2,1)S(1)}, bf16[1,64,1280]{2,1,0:T(8,128)(2,1)S(1)}, u32[]{:S(2)}, u32[]{:S(2)}) %collective-permute-start.7) | collective-permute-done | bytes 163872 | tf_op jit(solution)/shard_map/ppermute | solution.py:19
  166.4 4.7 %collective-permute-done.8 = bf16[1,64,1280]{2,1,0:T(8,128)(2,1)S(1)} collective-permute-done((bf16[1,64,1280]{2,1,0:T(8,128)(2,1)S(1)}, bf16[1,64,1280]{2,1,0:T(8,128)(2,1)S(1)}, u32[]{:S(2)}, u32[]{:S(2)}) %collective-permute-start.8) | collective-permute-done | bytes 163872 | tf_op jit(solution)/shard_map/ppermute | solution.py:19
  173.6 6.4 %collective-permute-done.9 = bf16[1,64,1280]{2,1,0:T(8,128)(2,1)S(1)} collective-permute-done((bf16[1,64,1280]{2,1,0:T(8,128)(2,1)S(1)}, bf16[1,64,1280]{2,1,0:T(8,128)(2,1)S(1)}, u32[]{:S(2)}, u32[]{:S(2)}) %collective-permute-start.9) | collective-permute-done | bytes 163872 | tf_op jit(solution)/shard_map/ppermute | solution.py:19
  180.0 4.3 collective-permute-start.10
  199.0 4.0 fusion.14
  204.9 22.7 %reduce-scatter.7.cloned.1.call-done = bf16[384,1024]{1,0:T(8,128)(2,1)} async-done(((bf16[768,1024]{1,0:T(8,128)(2,1)}), bf16[384,1024]{1,0:T(8,128)(2,1)}) %reduce-scatter.7.cloned.1.call-update) | async-done | bytes 786448
  229.0 27.5 %reduce-scatter.9.cloned.1.call-done = bf16[384,1024]{1,0:T(8,128)(2,1)} async-done(((bf16[768,1024]{1,0:T(8,128)(2,1)}), bf16[384,1024]{1,0:T(8,128)(2,1)}) %reduce-scatter.9.cloned.1.call-update) | async-done | bytes 786448
  259.9 27.3 %all-gather.3.cloned.1.call-done = bf16[1024,768]{1,0:T(8,128)(2,1)} async-done(((bf16[1024,384]{1,0:T(8,128)(2,1)}), bf16[1024,768]{1,0:T(8,128)(2,1)}) %all-gather.3.cloned.1.call-update) | async-done | bytes 1572880 | tf_op jit(solution)/shard_map/all_gather | solution.py:41
  287.3 5.1 %convolution_convert_fusion.1 = bf16[1024,1280]{1,0:T(8,128)(2,1)} fusion(bf16[1024,768]{1,0:T(8,128)(2,1)} %all-gather.3.cloned.1.call-done, bf16[1,768,1280]{2,1,0:T(8,128)(2,1)S(1)} %copy-done), kind=kOutput, calls=%fused_computation.14 | convolution fusion | flops 2014576640 | bytes 6160384 | tf_op jit(solution)/shard_map/dot_general | solution.py:85
  292.3 6.5 %all-to-all-start = ((bf16[16,64,1280]{2,1,0:T(8,128)(2,1)}), bf16[16,64,1280]{2,1,0:T(8,128)(2,1)S(1)}, u32[]{:S(2)}, u32[]{:S(2)}) async-start(bf16[16,64,1280]{2,1,0:T(8,128)(2,1)} %bitcast.65), calls=%async_computation | async-start | bytes 5242880 | tf_op jit(solution)/shard_map/all_to_all | solution.py:94
  299.4 28.8 %all-gather.5.cloned.1.call-done = bf16[1024,768]{1,0:T(8,128)(2,1)} async-done(((bf16[1024,384]{1,0:T(8,128)(2,1)}), bf16[1024,768]{1,0:T(8,128)(2,1)}) %all-gather.5.cloned.1.call-update) | async-done | bytes 1572880 | tf_op jit(solution)/shard_map/all_gather | solution.py:52
  328.2 5.8 %convolution_convert_fusion = bf16[1024,1280]{1,0:T(8,128)(2,1)} fusion(bf16[1024,768]{1,0:T(8,128)(2,1)} %all-gather.5.cloned.1.call-done, bf16[1,1280,768]{2,1,0:T(8,128)(2,1)} %param.12), kind=kOutput, calls=%fused_computation.13 | convolution fusion | flops 2014576640 | bytes 6160384 | tf_op jit(solution)/shard_map/dot_general | solution.py:104
  334.0 23.5 %all-to-all-done = bf16[16,64,1280]{2,1,0:T(8,128)(2,1)S(1)} async-done(((bf16[16,64,1280]{2,1,0:T(8,128)(2,1)}), bf16[16,64,1280]{2,1,0:T(8,128)(2,1)S(1)}, u32[]{:S(2)}, u32[]{:S(2)}) %all-to-all-start) | async-done | bytes 2621472 | tf_op jit(solution)/shard_map/all_to_all | solution.py:94
  357.5 4.8 %all-to-all-start.2 = ((bf16[16,64,1280]{2,1,0:T(8,128)(2,1)}), bf16[16,64,1280]{2,1,0:T(8,128)(2,1)}, u32[]{:S(2)}, u32[]{:S(2)}) async-start(bf16[16,64,1280]{2,1,0:T(8,128)(2,1)} %bitcast.66), calls=%async_computation.2 | async-start | bytes 5242880 | tf_op jit(solution)/shard_map/all_to_all | solution.py:112
  362.3 5.9 %fusion.1 = bf16[1,1280,768]{2,1,0:T(8,128)(2,1)} fusion(bf16[1024,1280]{1,0:T(8,128)(2,1)} %bitcast.68, bf16[1024,768]{1,0:T(8,128)(2,1)} %all-gather.5.cloned.1.call-done), kind=kOutput, calls=%fused_computation.17 | convolution fusion | flops 2014248960 | bytes 6160384 | tf_op jit(solution)/shard_map/dot_general | solution.py:101
  368.2 5.3 %fusion.2 = bf16[1,768,1280]{2,1,0:T(8,128)(2,1)} fusion(bf16[1024,768]{1,0:T(8,128)(2,1)S(1)} %copy-done.13, bf16[1024,1280]{1,0:T(8,128)(2,1)} %bitcast.8), kind=kOutput, calls=%fused_computation.18 | convolution fusion | flops 2014248960 | bytes 6160384 | tf_op jit(solution)/shard_map/dot_general | solution.py:98
  373.4 3.7 gather_fusion.1
  377.1 43.9 %all-to-all-done.2 = bf16[16,64,1280]{2,1,0:T(8,128)(2,1)} async-done(((bf16[16,64,1280]{2,1,0:T(8,128)(2,1)}), bf16[16,64,1280]{2,1,0:T(8,128)(2,1)}, u32[]{:S(2)}, u32[]{:S(2)}) %all-to-all-start.2) | async-done | bytes 2621472 | tf_op jit(solution)/shard_map/all_to_all | solution.py:112
  421.0 7.3 %gather_fusion.4 = bf16[768,1280]{1,0:T(8,128)(2,1)} fusion(bf16[1024,1280]{1,0:T(8,128)(2,1)} %bitcast.10, s32[1024]{0:T(1024)S(1)} %pad_clamp_fusion), kind=kCustom, calls=%fused_computation.4 | custom fusion | bytes 3935232 | tf_op jit(solution)/shard_map/gather | solution.py:116
  433.4 4.6 %reshape.104 = f32[128,6,1280]{2,1,0:T(8,128)} reshape(bf16[768,1280]{1,0:T(8,128)(2,1)} %gather_fusion.1) | data formatting | bytes 5898240 | tf_op jit(solution)/shard_map/convert_element_type | solution.py:116
  438.0 4.9 %multiply_reduce_fusion = bf16[128,1280]{1,0:T(8,128)(2,1)} fusion(f32[128,6,1280]{2,1,0:T(8,128)} %reshape.104, f32[128,6]{1,0:T(8,128)S(1)} %copy-done.5), kind=kLoop, calls=%fused_computation.12 | loop fusion | flops 1802240 | bytes 4262912 | tf_op jit(solution)/shard_map/reduce_sum | solution.py:118
  (106 shorter events, 60.8 us)
Async XLA Ops:
  7.2 191.8 %copy-start = (bf16[1,768,1280]{2,1,0:T(8,128)(2,1)S(1)}, bf16[1,768,1280]{2,1,0:T(8,128)(2,1)}, u32[]{:S(2)}) copy-start(bf16[1,768,1280]{2,1,0:T(8,128)(2,1)} %param.13) | copy-start | bytes 5898244
  26.8 6.2 %copy-start.6 = (bf16[128,1280]{1,0:T(8,128)(2,1)S(1)}, bf16[128,1280]{1,0:T(8,128)(2,1)}, u32[]{:S(2)}) copy-start(bf16[128,1280]{1,0:T(8,128)(2,1)} %param.9) | copy-start | bytes 983044
  26.8 27.9 %collective-permute-start = (bf16[1,64,1280]{2,1,0:T(8,128)(2,1)}, bf16[1,64,1280]{2,1,0:T(8,128)(2,1)}, u32[]{:S(2)}, u32[]{:S(2)}) collective-permute-start(bf16[1,64,1280]{2,1,0:T(8,128)(2,1)} %get-tuple-element.19), channel_id=1, source_target_pairs={{0,15},{1,0},{2,1},{3,2},{4,3},{5,4},{6,5},{7,6},{8,7},{9,8},{10,9... | collective-permute-start | bytes 491528 | tf_op jit(solution)/shard_map/ppermute | solution.py:19
  42.2 101.7 %copy-start.10 = (bf16[1,64,1280]{2,1,0:T(8,128)(2,1)S(1)}, bf16[1,64,1280]{2,1,0:T(8,128)(2,1)}, u32[]{:S(2)}) copy-start(bf16[1,64,1280]{2,1,0:T(8,128)(2,1)} %get-tuple-element.13) | copy-start | bytes 491524
  42.2 108.3 %copy-start.9 = (bf16[1,64,1280]{2,1,0:T(8,128)(2,1)S(1)}, bf16[1,64,1280]{2,1,0:T(8,128)(2,1)}, u32[]{:S(2)}) copy-start(bf16[1,64,1280]{2,1,0:T(8,128)(2,1)} %get-tuple-element.12) | copy-start | bytes 491524
  42.2 120.8 %copy-start.8 = (bf16[1,64,1280]{2,1,0:T(8,128)(2,1)S(1)}, bf16[1,64,1280]{2,1,0:T(8,128)(2,1)}, u32[]{:S(2)}) copy-start(bf16[1,64,1280]{2,1,0:T(8,128)(2,1)} %get-tuple-element.11) | copy-start | bytes 491524
  42.2 156.8 %all-to-all-start.1 = ((bf16[16,64,1280]{2,1,0:T(8,128)(2,1)}), bf16[16,64,1280]{2,1,0:T(8,128)(2,1)}, u32[]{:S(2)}, u32[]{:S(2)}) async-start(bf16[16,64,1280]{2,1,0:T(8,128)(2,1)} %fusion), calls=%async_computation.1 | async-start | bytes 5242880 | tf_op jit(solution)/shard_map/all_to_all | solution.py:95
  50.7 120.4 %copy-start.7 = (bf16[1,64,1280]{2,1,0:T(8,128)(2,1)S(1)}, bf16[1,64,1280]{2,1,0:T(8,128)(2,1)}, u32[]{:S(2)}) copy-start(bf16[1,64,1280]{2,1,0:T(8,128)(2,1)} %get-tuple-element.10) | copy-start | bytes 491524
  50.7 176.9 %reduce-scatter.7.cloned.1.call-start = ((), (), s32[]{:S(2)}) async-start(), calls=%async_computation.7 | async-start | bytes 2359296
  50.7 140.0 %collective-permute-start.14 = (bf16[1,64,1280]{2,1,0:T(8,128)(2,1)S(1)}, bf16[1,64,1280]{2,1,0:T(8,128)(2,1)}, u32[]{:S(2)}, u32[]{:S(2)}) collective-permute-start(bf16[1,64,1280]{2,1,0:T(8,128)(2,1)S(1)} %get-tuple-element.5), channel_id=1, source_target_pairs={{0,1},{1,2},{2,3},{3,4},{4,5},{5,6},{6,7},{7,8},{8,9},{9,10},{10,1... | collective-permute-start | bytes 491528 | tf_op jit(solution)/shard_map/ppermute | solution.py:19
  52.3 137.5 %collective-permute-start.13 = (bf16[1,64,1280]{2,1,0:T(8,128)(2,1)S(1)}, bf16[1,64,1280]{2,1,0:T(8,128)(2,1)}, u32[]{:S(2)}, u32[]{:S(2)}) collective-permute-start(bf16[1,64,1280]{2,1,0:T(8,128)(2,1)S(1)} %get-tuple-element.6), channel_id=1, source_target_pairs={{0,2},{1,3},{2,4},{3,5},{4,6},{5,7},{6,8},{7,9},{8,10},{9,11},{10,... | collective-permute-start | bytes 491528 | tf_op jit(solution)/shard_map/ppermute | solution.py:19
  53.5 135.4 %collective-permute-start.12 = (bf16[1,64,1280]{2,1,0:T(8,128)(2,1)S(1)}, bf16[1,64,1280]{2,1,0:T(8,128)(2,1)}, u32[]{:S(2)}, u32[]{:S(2)}) collective-permute-start(bf16[1,64,1280]{2,1,0:T(8,128)(2,1)S(1)} %get-tuple-element.7), channel_id=1, source_target_pairs={{0,3},{1,4},{2,5},{3,6},{4,7},{5,8},{6,9},{7,10},{8,11},{9,12},{10... | collective-permute-start | bytes 491528 | tf_op jit(solution)/shard_map/ppermute | solution.py:19
  53.9 134.0 %collective-permute-start.11 = (bf16[1,64,1280]{2,1,0:T(8,128)(2,1)S(1)}, bf16[1,64,1280]{2,1,0:T(8,128)(2,1)}, u32[]{:S(2)}, u32[]{:S(2)}) collective-permute-start(bf16[1,64,1280]{2,1,0:T(8,128)(2,1)S(1)} %get-tuple-element.8), channel_id=1, source_target_pairs={{0,4},{1,5},{2,6},{3,7},{4,8},{5,9},{6,10},{7,11},{8,12},{9,13},{1... | collective-permute-start | bytes 491528 | tf_op jit(solution)/shard_map/ppermute | solution.py:19
  54.7 63.2 %collective-permute-start.1 = (bf16[1,64,1280]{2,1,0:T(8,128)(2,1)}, bf16[1,64,1280]{2,1,0:T(8,128)(2,1)S(1)}, u32[]{:S(2)}, u32[]{:S(2)}) collective-permute-start(bf16[1,64,1280]{2,1,0:T(8,128)(2,1)} %get-tuple-element.18), channel_id=1, source_target_pairs={{0,14},{1,15},{2,0},{3,1},{4,2},{5,3},{6,4},{7,5},{8,6},{9,7},{10,... | collective-permute-start | bytes 491528 | tf_op jit(solution)/shard_map/ppermute | solution.py:19
  117.9 5.8 %collective-permute-start.2 = (bf16[1,64,1280]{2,1,0:T(8,128)(2,1)}, bf16[1,64,1280]{2,1,0:T(8,128)(2,1)S(1)}, u32[]{:S(2)}, u32[]{:S(2)}) collective-permute-start(bf16[1,64,1280]{2,1,0:T(8,128)(2,1)} %get-tuple-element.17), channel_id=1, source_target_pairs={{0,13},{1,14},{2,15},{3,0},{4,1},{5,2},{6,3},{7,4},{8,5},{9,6},{10... | collective-permute-start | bytes 491528 | tf_op jit(solution)/shard_map/ppermute | solution.py:19
  123.7 4.9 %collective-permute-start.3 = (bf16[1,64,1280]{2,1,0:T(8,128)(2,1)}, bf16[1,64,1280]{2,1,0:T(8,128)(2,1)S(1)}, u32[]{:S(2)}, u32[]{:S(2)}) collective-permute-start(bf16[1,64,1280]{2,1,0:T(8,128)(2,1)} %get-tuple-element.16), channel_id=1, source_target_pairs={{0,12},{1,13},{2,14},{3,15},{4,0},{5,1},{6,2},{7,3},{8,4},{9,5},{1... | collective-permute-start | bytes 491528 | tf_op jit(solution)/shard_map/ppermute | solution.py:19
  128.6 7.7 %collective-permute-start.4 = (bf16[1,64,1280]{2,1,0:T(8,128)(2,1)}, bf16[1,64,1280]{2,1,0:T(8,128)(2,1)S(1)}, u32[]{:S(2)}, u32[]{:S(2)}) collective-permute-start(bf16[1,64,1280]{2,1,0:T(8,128)(2,1)} %get-tuple-element.15), channel_id=1, source_target_pairs={{0,11},{1,12},{2,13},{3,14},{4,15},{5,0},{6,1},{7,2},{8,3},{9,4},{... | collective-permute-start | bytes 491528 | tf_op jit(solution)/shard_map/ppermute | solution.py:19
  136.3 7.6 %collective-permute-start.5 = (bf16[1,64,1280]{2,1,0:T(8,128)(2,1)}, bf16[1,64,1280]{2,1,0:T(8,128)(2,1)S(1)}, u32[]{:S(2)}, u32[]{:S(2)}) collective-permute-start(bf16[1,64,1280]{2,1,0:T(8,128)(2,1)} %get-tuple-element.14), channel_id=1, source_target_pairs={{0,10},{1,11},{2,12},{3,13},{4,14},{5,15},{6,0},{7,1},{8,2},{9,3},... | collective-permute-start | bytes 491528 | tf_op jit(solution)/shard_map/ppermute | solution.py:19
  144.0 6.5 %collective-permute-start.6 = (bf16[1,64,1280]{2,1,0:T(8,128)(2,1)S(1)}, bf16[1,64,1280]{2,1,0:T(8,128)(2,1)S(1)}, u32[]{:S(2)}, u32[]{:S(2)}) collective-permute-start(bf16[1,64,1280]{2,1,0:T(8,128)(2,1)S(1)} %copy-done.10), channel_id=1, source_target_pairs={{0,9},{1,10},{2,11},{3,12},{4,13},{5,14},{6,15},{7,0},{8,1},{9,2},... | collective-permute-start | bytes 491528 | tf_op jit(solution)/shard_map/ppermute | solution.py:19
  150.5 12.5 %collective-permute-start.7 = (bf16[1,64,1280]{2,1,0:T(8,128)(2,1)S(1)}, bf16[1,64,1280]{2,1,0:T(8,128)(2,1)S(1)}, u32[]{:S(2)}, u32[]{:S(2)}) collective-permute-start(bf16[1,64,1280]{2,1,0:T(8,128)(2,1)S(1)} %copy-done.9), channel_id=1, source_target_pairs={{0,8},{1,9},{2,10},{3,11},{4,12},{5,13},{6,14},{7,15},{8,0},{9,1},... | collective-permute-start | bytes 491528 | tf_op jit(solution)/shard_map/ppermute | solution.py:19
  163.0 8.1 %collective-permute-start.8 = (bf16[1,64,1280]{2,1,0:T(8,128)(2,1)S(1)}, bf16[1,64,1280]{2,1,0:T(8,128)(2,1)S(1)}, u32[]{:S(2)}, u32[]{:S(2)}) collective-permute-start(bf16[1,64,1280]{2,1,0:T(8,128)(2,1)S(1)} %copy-done.8), channel_id=1, source_target_pairs={{0,7},{1,8},{2,9},{3,10},{4,11},{5,12},{6,13},{7,14},{8,15},{9,0},... | collective-permute-start | bytes 491528 | tf_op jit(solution)/shard_map/ppermute | solution.py:19
  171.1 8.9 %collective-permute-start.9 = (bf16[1,64,1280]{2,1,0:T(8,128)(2,1)S(1)}, bf16[1,64,1280]{2,1,0:T(8,128)(2,1)S(1)}, u32[]{:S(2)}, u32[]{:S(2)}) collective-permute-start(bf16[1,64,1280]{2,1,0:T(8,128)(2,1)S(1)} %copy-done.7), channel_id=1, source_target_pairs={{0,6},{1,7},{2,8},{3,9},{4,10},{5,11},{6,12},{7,13},{8,14},{9,15},... | collective-permute-start | bytes 491528 | tf_op jit(solution)/shard_map/ppermute | solution.py:19
  180.0 7.9 %collective-permute-start.10 = (bf16[1,64,1280]{2,1,0:T(8,128)(2,1)S(1)}, bf16[1,64,1280]{2,1,0:T(8,128)(2,1)S(1)}, u32[]{:S(2)}, u32[]{:S(2)}) collective-permute-start(bf16[1,64,1280]{2,1,0:T(8,128)(2,1)S(1)} %get-tuple-element.9), channel_id=1, source_target_pairs={{0,5},{1,6},{2,7},{3,8},{4,9},{5,10},{6,11},{7,12},{8,13},{9,14},{... | collective-permute-start | bytes 491528 | tf_op jit(solution)/shard_map/ppermute | solution.py:19
  192.6 2.5 copy-start.12
  198.9 57.6 %reduce-scatter.9.cloned.1.call-start = ((), (), s32[]{:S(2)}) async-start(), calls=%async_computation.8 | async-start | bytes 2359296
  204.6 82.6 %all-gather.3.cloned.1.call-start = ((), (), s32[]{:S(2)}) async-start(), calls=%async_computation.5 | async-start | bytes 2359296 | tf_op jit(solution)/shard_map/all_gather | solution.py:41
  292.3 65.2 %all-to-all-start = ((bf16[16,64,1280]{2,1,0:T(8,128)(2,1)}), bf16[16,64,1280]{2,1,0:T(8,128)(2,1)S(1)}, u32[]{:S(2)}, u32[]{:S(2)}) async-start(bf16[16,64,1280]{2,1,0:T(8,128)(2,1)} %bitcast.65), calls=%async_computation | async-start | bytes 5242880 | tf_op jit(solution)/shard_map/all_to_all | solution.py:94
  298.8 29.3 %all-gather.5.cloned.1.call-start = ((), (), s32[]{:S(2)}) async-start(), calls=%async_computation.6 | async-start | bytes 2359296 | tf_op jit(solution)/shard_map/all_gather | solution.py:52
  357.5 63.5 %all-to-all-start.2 = ((bf16[16,64,1280]{2,1,0:T(8,128)(2,1)}), bf16[16,64,1280]{2,1,0:T(8,128)(2,1)}, u32[]{:S(2)}, u32[]{:S(2)}) async-start(bf16[16,64,1280]{2,1,0:T(8,128)(2,1)} %bitcast.66), calls=%async_computation.2 | async-start | bytes 5242880 | tf_op jit(solution)/shard_map/all_to_all | solution.py:112
  362.3 5.9 %copy-start.13 = (bf16[1024,768]{1,0:T(8,128)(2,1)S(1)}, bf16[1024,768]{1,0:T(8,128)(2,1)}, u32[]{:S(2)}) copy-start(bf16[1024,768]{1,0:T(8,128)(2,1)} %all-gather.3.cloned.1.call-done) | copy-start | bytes 4718596
  433.4 4.6 %copy-start.5 = (f32[128,6]{1,0:T(8,128)S(1)}, f32[128,6]{1,0:T(8,128)}, u32[]{:S(2)}) copy-start(f32[128,6]{1,0:T(8,128)} %copy-done.4) | copy-start | bytes 9220
  433.4 9.5 %copy-start.1 = (bf16[1,768,1280]{2,1,0:T(8,128)(2,1)S(1)}, bf16[1,768,1280]{2,1,0:T(8,128)(2,1)}, u32[]{:S(2)}) copy-start(bf16[1,768,1280]{2,1,0:T(8,128)(2,1)} %param.13) | copy-start | bytes 5898244
  (4 other events, 5.5 us)
Sparse Core Ops, SparseCore 0:
  199.1 28.4 reduce-scatter.6
  230.4 26.1 reduce-scatter.8
  260.1 27.1 all-gather.2
  301.5 26.6 all-gather.4
